TPU v7x, 32 devices: a whole 2x2x4 slice. The times are simulated.
32 devices in a mesh: fsdp: 8 (over z, y), tensor: 4 (over x, core).
Axes of the slice: x: 2, y: 2, z: 4, core: 2. Of those that a mesh axis runs over, the one named last changes fastest.
Arguments:
- images: bfloat16 [2, 8, 577, 1024], P(None, 'fsdp'), may hold values from -6 to 6
- cotangent: bfloat16 [2, 8, 577, 1024], P(None, 'fsdp'), may hold values from -6 to 6
- ln1_gain: bfloat16 [1024], P(('fsdp', 'tensor')), may hold values from 0.5 to 1.5
- ln1_bias: bfloat16 [1024], P(('fsdp', 'tensor')), may hold values from -3 to 3
- qkv_weight: bfloat16 [1024, 16, 192], P('fsdp', 'tensor'), may hold values from -0.1875 to 0.1875
- qv_bias: bfloat16 [16, 128], P('tensor', 'fsdp'), may hold values from -1.1953125 to 1.1953125
- out_weight: bfloat16 [1024, 1024], P('tensor', 'fsdp'), may hold values from -0.75 to 0.75
- out_bias: bfloat16 [1024], P(('fsdp', 'tensor')), may hold values from -3 to 3
- ln2_gain: bfloat16 [1024], P(('fsdp', 'tensor')), may hold values from 0.5 to 1.5
- ln2_bias: bfloat16 [1024], P(('fsdp', 'tensor')), may hold values from -3 to 3
- up_weight: bfloat16 [1024, 4096], P('fsdp', 'tensor'), may hold values from -0.1875 to 0.1875
- up_bias: bfloat16 [4, 1024], P('tensor', 'fsdp'), may hold values from -3 to 3
- down_weight: bfloat16 [4096, 1024], P('tensor', 'fsdp'), may hold values from -0.09375 to 0.09375
- down_bias: bfloat16 [1024], P(('fsdp', 'tensor')), may hold values from -3 to 3
Outputs:
- activations: bfloat16 [2, 8, 577, 1024], P(None, 'fsdp')
- input_grad: float32 [2, 8, 577, 1024], P(None, 'fsdp')
- ln1_gain_grad: float32 [1024], P(('fsdp', 'tensor'))
- ln1_bias_grad: float32 [1024], P(('fsdp', 'tensor'))
- qkv_weight_grad: float32 [1024, 16, 192], P('fsdp', 'tensor')
- qv_bias_grad: float32 [16, 128], P('tensor', 'fsdp')
- out_weight_grad: float32 [1024, 1024], P('tensor', 'fsdp')
- out_bias_grad: float32 [1024], P(('fsdp', 'tensor'))
- ln2_gain_grad: float32 [1024], P(('fsdp', 'tensor'))
- ln2_bias_grad: float32 [1024], P(('fsdp', 'tensor'))
- up_weight_grad: float32 [1024, 4096], P('fsdp', 'tensor')
- up_bias_grad: float32 [4, 1024], P('tensor', 'fsdp')
- down_weight_grad: float32 [4096, 1024], P('tensor', 'fsdp')
- down_bias_grad: float32 [1024], P(('fsdp', 'tensor'))
All inputs are finite; a program needn't handle non-finite values.
Results may differ from a plain program's by a relative error of at most 0.023.
Values may be sent and summed in bfloat16 or wider, within the bound.
No kernel may reach another device: no remote copies, remote signals or barrier semaphores. Data moves between devices by JAX's collectives and lax.ppermute only.
A program may use at most 128 MiB of HBM per device.

v0:
```python
import jax
import jax.numpy as jnp
from jax import lax
from jax.sharding import PartitionSpec as P

epsilon = 1e-06


def layer_norm(values, scale_vec, shift_vec):
    centred = values - jnp.mean(values, axis=-1, keepdims=True)
    spread = jnp.mean(centred * centred, axis=-1, keepdims=True)
    return centred * lax.rsqrt(spread + epsilon) * scale_vec + shift_vec


def gelu_exact(values):
    return jax.nn.gelu(values, approximate=False)


def unpack_attn(gathered, model_width):
    qkv_full, qv_full, out_full = gathered
    return (qkv_full.reshape(model_width, -1), qv_full.astype(jnp.float32), out_full)


def unpack_mlp(gathered):
    up_full, up_shift_full, down_full = gathered
    return (up_full, up_shift_full.reshape(-1).astype(jnp.float32), down_full)


def shards(
    images,
    cotangent,
    ln1_gain,
    ln1_bias,
    qkv_weight,
    qv_bias,
    out_weight,
    out_bias,
    ln2_gain,
    ln2_bias,
    up_weight,
    up_bias,
    down_weight,
    down_bias,
):
    micro_count, images_local, seq_len, model_width = images.shape
    row_count = images_local * seq_len
    heads_local = qkv_weight.shape[1]
    head_dim = qkv_weight.shape[2] // 3
    qkv_cols = heads_local * 3 * head_dim
    hidden_local = up_weight.shape[1]
    score_scale = head_dim ** (-0.5)
    fsdp_count = lax.axis_size("fsdp")
    tensor_count = lax.axis_size("tensor")
    f32 = jnp.float32
    bf16 = jnp.bfloat16
    vector_list = (
        lax.all_gather(ln1_gain, ("fsdp", "tensor"), axis=0, tiled=True),
        lax.all_gather(ln1_bias, ("fsdp", "tensor"), axis=0, tiled=True),
        lax.all_gather(out_bias, ("fsdp", "tensor"), axis=0, tiled=True),
        lax.all_gather(ln2_gain, ("fsdp", "tensor"), axis=0, tiled=True),
        lax.all_gather(ln2_bias, ("fsdp", "tensor"), axis=0, tiled=True),
        lax.all_gather(down_bias, ("fsdp", "tensor"), axis=0, tiled=True),
    )
    gain_one, shift_one, out_shift, gain_two, shift_two, down_shift = [
        member.astype(f32) for member in vector_list
    ]
    qkv_acc = jnp.zeros((model_width, qkv_cols), f32)
    qv_acc = jnp.zeros((heads_local, 2 * head_dim), f32)
    out_acc = jnp.zeros((heads_local * head_dim, model_width), f32)
    up_acc = jnp.zeros((model_width, hidden_local), f32)
    up_shift_acc = jnp.zeros((hidden_local,), f32)
    down_acc = jnp.zeros((hidden_local, model_width), f32)
    gain_one_acc = jnp.zeros((model_width,), f32)
    shift_one_acc = jnp.zeros((model_width,), f32)
    out_shift_acc = jnp.zeros((model_width,), f32)
    gain_two_acc = jnp.zeros((model_width,), f32)
    shift_two_acc = jnp.zeros((model_width,), f32)
    down_shift_acc = jnp.zeros((model_width,), f32)
    outputs_all = []
    grads_in_all = []
    for mb_index in range(micro_count):
        attn_full = (
            lax.all_gather(qkv_weight, "fsdp", axis=0, tiled=True),
            lax.all_gather(qv_bias, "fsdp", axis=1, tiled=True),
            lax.all_gather(out_weight, "fsdp", axis=1, tiled=True),
        )
        qkv_mat, qv_shift, out_mat = unpack_attn(attn_full, model_width)
        input_rows = images[mb_index].reshape(row_count, model_width).astype(f32)
        normed_one, norm_one_pull = jax.vjp(layer_norm, input_rows, gain_one, shift_one)
        act_one = normed_one.astype(bf16)
        projected = jnp.dot(act_one, qkv_mat, preferred_element_type=f32).reshape(
            images_local, seq_len, heads_local, 3 * head_dim
        )
        queries = (projected[..., :head_dim] + qv_shift[:, :head_dim]).astype(bf16)
        key_rows = projected[..., head_dim : 2 * head_dim].astype(bf16)
        val_rows = (projected[..., 2 * head_dim :] + qv_shift[:, head_dim:]).astype(bf16)
        scores = (
            jnp.einsum("bshd,bthd->bhst", queries, key_rows, preferred_element_type=f32)
            * score_scale
        )
        top_score = jnp.max(scores, axis=-1, keepdims=True)
        exp_scores = jnp.exp(scores - top_score)
        exp_total = jnp.sum(exp_scores, axis=-1, keepdims=True)
        logsum_exp = top_score + jnp.log(exp_total)
        weights_low = (exp_scores / exp_total).astype(bf16)
        attended = (
            jnp.einsum("bhst,bthd->bshd", weights_low, val_rows, preferred_element_type=f32)
            .astype(bf16)
            .reshape(row_count, heads_local * head_dim)
        )
        branch_part = jnp.dot(attended, out_mat, preferred_element_type=f32)
        hidden_res = input_rows + (
            lax.psum(branch_part.astype(jnp.bfloat16), "tensor").astype(jnp.float32) + out_shift
        )
        mlp_full = (
            lax.all_gather(up_weight, "fsdp", axis=0, tiled=True),
            lax.all_gather(up_bias, "fsdp", axis=1, tiled=True),
            lax.all_gather(down_weight, "fsdp", axis=1, tiled=True),
        )
        up_mat, up_shift, down_mat = unpack_mlp(mlp_full)
        normed_two, norm_two_pull = jax.vjp(layer_norm, hidden_res, gain_two, shift_two)
        act_two = normed_two.astype(bf16)
        pre_act = jnp.dot(act_two, up_mat, preferred_element_type=f32) + up_shift
        gelu_full, gelu_pull = jax.vjp(gelu_exact, pre_act)
        activated = gelu_full.astype(bf16)
        mlp_part = jnp.dot(activated, down_mat, preferred_element_type=f32)
        mlp_total = lax.psum(mlp_part.astype(jnp.bfloat16), "tensor").astype(jnp.float32)
        output_rows = (hidden_res + (mlp_total + down_shift)).astype(bf16)
        outputs_all.append(output_rows.reshape(images_local, seq_len, model_width))
        up_mat, up_shift, down_mat = unpack_mlp(
            (
                lax.all_gather(up_weight, "fsdp", axis=0, tiled=True),
                lax.all_gather(up_bias, "fsdp", axis=1, tiled=True),
                lax.all_gather(down_weight, "fsdp", axis=1, tiled=True),
            )
        )
        grad_mlp = cotangent[mb_index].reshape(row_count, model_width)
        grad_out = grad_mlp.astype(f32)
        down_shift_acc = down_shift_acc + jnp.sum(grad_out, axis=0)
        down_acc = down_acc + jnp.einsum(
            "rf,rd->fd", activated, grad_mlp, preferred_element_type=f32
        )
        grad_act = jnp.einsum("rd,fd->rf", grad_mlp, down_mat, preferred_element_type=f32)
        grad_pre = gelu_pull(grad_act)[0].astype(bf16)
        up_shift_acc = up_shift_acc + jnp.sum(grad_pre.astype(f32), axis=0)
        up_acc = up_acc + jnp.einsum("rd,rf->df", act_two, grad_pre, preferred_element_type=f32)
        grad_two = lax.psum(
            jnp.einsum("rf,df->rd", grad_pre, up_mat, preferred_element_type=f32).astype(
                jnp.bfloat16
            ),
            "tensor",
        ).astype(jnp.float32)
        grad_norm_in, gain_two_step, shift_two_step = norm_two_pull(grad_two)
        gain_two_acc = gain_two_acc + gain_two_step
        shift_two_acc = shift_two_acc + shift_two_step
        grad_hidden = grad_out + grad_norm_in
        qkv_mat, qv_shift, out_mat = unpack_attn(
            (
                lax.all_gather(qkv_weight, "fsdp", axis=0, tiled=True),
                lax.all_gather(qv_bias, "fsdp", axis=1, tiled=True),
                lax.all_gather(out_weight, "fsdp", axis=1, tiled=True),
            ),
            model_width,
        )
        grad_branch = grad_hidden.astype(bf16)
        out_shift_acc = out_shift_acc + jnp.sum(grad_branch.astype(f32), axis=0)
        out_acc = out_acc + jnp.einsum(
            "ra,rd->ad", attended, grad_branch, preferred_element_type=f32
        )
        grad_att = (
            jnp.einsum("rd,ad->ra", grad_branch, out_mat, preferred_element_type=f32)
            .astype(bf16)
            .reshape(images_local, seq_len, heads_local, head_dim)
        )
        again_scores = (
            jnp.einsum("bshd,bthd->bhst", queries, key_rows, preferred_element_type=f32)
            * score_scale
        )
        probs_full = jnp.exp(again_scores - logsum_exp)
        probs_low = probs_full.astype(bf16)
        val_grad = jnp.einsum(
            "bhst,bshd->bthd", probs_low, grad_att, preferred_element_type=f32
        ).astype(bf16)
        prob_grad = jnp.einsum("bshd,bthd->bhst", grad_att, val_rows, preferred_element_type=f32)
        inner_sum = jnp.sum(prob_grad * probs_full, axis=-1, keepdims=True)
        score_grad = (probs_full * (prob_grad - inner_sum)).astype(bf16)
        query_grad = (
            jnp.einsum("bhst,bthd->bshd", score_grad, key_rows, preferred_element_type=f32)
            * score_scale
        ).astype(bf16)
        key_grad = (
            jnp.einsum("bhst,bshd->bthd", score_grad, queries, preferred_element_type=f32)
            * score_scale
        ).astype(bf16)
        qv_step = jnp.concatenate(
            [
                jnp.sum(query_grad.astype(f32), axis=(0, 1)),
                jnp.sum(val_grad.astype(f32), axis=(0, 1)),
            ],
            axis=-1,
        )
        qv_acc = qv_acc + qv_step
        grad_proj = jnp.concatenate([query_grad, key_grad, val_grad], axis=-1).reshape(
            row_count, qkv_cols
        )
        qkv_acc = qkv_acc + jnp.einsum("rd,rc->dc", act_one, grad_proj, preferred_element_type=f32)
        grad_one = lax.psum(
            jnp.einsum("rc,dc->rd", grad_proj, qkv_mat, preferred_element_type=f32).astype(
                jnp.bfloat16
            ),
            "tensor",
        ).astype(jnp.float32)
        grad_input_ln, gain_one_step, shift_one_step = norm_one_pull(grad_one)
        gain_one_acc = gain_one_acc + gain_one_step
        shift_one_acc = shift_one_acc + shift_one_step
        grads_in_all.append(
            (grad_hidden + grad_input_ln).reshape(images_local, seq_len, model_width)
        )
    owned = (
        lax.psum_scatter(
            qkv_acc.reshape(model_width, heads_local, 3 * head_dim).astype(jnp.bfloat16),
            "fsdp",
            scatter_dimension=0,
            tiled=True,
        ).astype(jnp.float32),
        lax.psum_scatter(
            qv_acc.astype(jnp.bfloat16), "fsdp", scatter_dimension=1, tiled=True
        ).astype(jnp.float32),
        lax.psum_scatter(
            out_acc.astype(jnp.bfloat16), "fsdp", scatter_dimension=1, tiled=True
        ).astype(jnp.float32),
        lax.psum_scatter(
            up_acc.astype(jnp.bfloat16), "fsdp", scatter_dimension=0, tiled=True
        ).astype(jnp.float32),
        lax.psum_scatter(
            up_shift_acc.reshape(1, hidden_local).astype(jnp.bfloat16),
            "fsdp",
            scatter_dimension=1,
            tiled=True,
        ).astype(jnp.float32),
        lax.psum_scatter(
            down_acc.astype(jnp.bfloat16), "fsdp", scatter_dimension=1, tiled=True
        ).astype(jnp.float32),
        lax.psum_scatter(
            gain_one_acc.astype(jnp.bfloat16), "fsdp", scatter_dimension=0, tiled=True
        ).astype(jnp.float32),
        lax.psum_scatter(
            shift_one_acc.astype(jnp.bfloat16), "fsdp", scatter_dimension=0, tiled=True
        ).astype(jnp.float32),
        lax.psum_scatter(
            out_shift_acc.astype(jnp.bfloat16), "fsdp", scatter_dimension=0, tiled=True
        ).astype(jnp.float32),
        lax.psum_scatter(
            gain_two_acc.astype(jnp.bfloat16), "fsdp", scatter_dimension=0, tiled=True
        ).astype(jnp.float32),
        lax.psum_scatter(
            shift_two_acc.astype(jnp.bfloat16), "fsdp", scatter_dimension=0, tiled=True
        ).astype(jnp.float32),
        lax.psum_scatter(
            down_shift_acc.astype(jnp.bfloat16), "fsdp", scatter_dimension=0, tiled=True
        ).astype(jnp.float32),
    )
    piece_len = model_width // (fsdp_count * tensor_count)
    piece_start = lax.axis_index("tensor") * piece_len
    vector_grads = [
        lax.dynamic_slice_in_dim(member, piece_start, piece_len, 0) for member in owned[6:]
    ]
    activations = jnp.stack(outputs_all, axis=0)
    input_grad = jnp.stack(grads_in_all, axis=0)
    return (
        activations,
        input_grad,
        vector_grads[0],
        vector_grads[1],
        owned[0],
        owned[1],
        owned[2],
        vector_grads[2],
        vector_grads[3],
        vector_grads[4],
        owned[3],
        owned[4],
        owned[5],
        vector_grads[5],
    )


def solution(mesh):
    return jax.shard_map(
        shards,
        mesh=mesh,
        in_specs=(
            P(None, "fsdp", None, None),
            P(None, "fsdp", None, None),
            P(("fsdp", "tensor")),
            P(("fsdp", "tensor")),
            P("fsdp", "tensor", None),
            P("tensor", "fsdp"),
            P("tensor", "fsdp"),
            P(("fsdp", "tensor")),
            P(("fsdp", "tensor")),
            P(("fsdp", "tensor")),
            P("fsdp", "tensor"),
            P("tensor", "fsdp"),
            P("tensor", "fsdp"),
            P(("fsdp", "tensor")),
        ),
        out_specs=(
            P(None, "fsdp", None, None),
            P(None, "fsdp", None, None),
            P(("fsdp", "tensor")),
            P(("fsdp", "tensor")),
            P("fsdp", "tensor", None),
            P("tensor", "fsdp"),
            P("tensor", "fsdp"),
            P(("fsdp", "tensor")),
            P(("fsdp", "tensor")),
            P(("fsdp", "tensor")),
            P("fsdp", "tensor"),
            P("tensor", "fsdp"),
            P("tensor", "fsdp"),
            P(("fsdp", "tensor")),
        ),
        check_vma=False,
    )
```

profile of v0, /device:TPU:0, one launch (start us, length us, event | category | flops | bytes accessed | tf_op | source)
XLA Modules:
  0.0 895.7 jit_solution(1121077081818013780)
XLA Ops:
  13.0 43.2 %all-reduce.12 = (bf16[1024]{0:T(1024)(128)(2,1)S(1)}, bf16[1024]{0:T(1024)(128)(2,1)S(1)}, bf16[1024]{0:T(1024)(128)(2,1)S(1)}, bf16[1024]{0:T(1024)(128)(2,1)S...) all-reduce(bf16[1024]{0:T(1024)(128)(2,1)S(1)} %dynamic-update-slic, ...), channel_id=1, replica_groups=mesh['fsdp'=8,'tensor'=4] {'fsdp','tensor'}, use_global_device_ids=true, to_apply=%add.1 | all-reduce | flops 6144 | bytes 24576
  56.2 21.0 %all-gather = bf16[8,16,4]{1,2,0:T(4,128)(2,1)S(1)} all-gather(bf16[1,16,4]{1,2,0:T(4,128)(2,1)} %bitcast.357), channel_id=1, replica_groups=mesh['fsdp'=8,'tensor'=4] {'fsdp'}, dimensions={0}, use_global_device_ids=true | all-gather | bytes 1152 | tf_op jit(solution)/shard_map/all_gather | solution.py:84
  77.2 6.4 fusion.181
  85.6 27.5 %all_gather.54 = bf16[256,1024]{1,0:T(8,128)(2,1)S(1)} all-gather(bf16[256,128]{1,0:T(8,128)(2,1)S(1)} %copy-done.45), channel_id=1, replica_groups=mesh['fsdp'=8,'tensor'=4] {'fsdp'}, dimensions={1}, use_global_device_ids=true | all-gather | bytes 589824 | tf_op jit(solution)/shard_map/all_gather | solution.py:85
  131.0 16.7 %all_gather.59 = bf16[1,1024]{1,0:T(2,128)(2,1)S(1)} all-gather(bf16[1,128]{1,0:T(2,128)(2,1)S(1)} %copy-done.57), channel_id=1, replica_groups=mesh['fsdp'=8,'tensor'=4] {'fsdp'}, dimensions={1}, use_global_device_ids=true | all-gather | bytes 2304 | tf_op jit(solution)/shard_map/all_gather | solution.py:117
  147.6 6.5 fusion.180
  157.4 25.4 %all-reduce.27.cloned.1.call-done = (bf16[577,1024]{1,0:T(8,128)(2,1)}, bf16[577,1024]{1,0:T(8,128)(2,1)}) async-done(((bf16[577,1024]{1,0:T(8,128)(2,1)}, bf16[577,1024]{1,0:T(8,128)(2,1)}), (bf16[577,1024]{1,0:T(8,128)(2,1)}, bf16[577,1024]{1,0:T(8,128)(2,1)})) %all-reduce.27.cloned.1.call-update) | async-done | bytes 2363408 | tf_op jit(solution)/shard_map/psum | solution.py:113
  186.1 48.1 %all-gather.7.cloned.1.call-done = bf16[1024,1024]{1,0:T(8,128)(2,1)} async-done(((bf16[128,1024]{1,0:T(8,128)(2,1)}), bf16[1024,1024]{1,0:T(8,128)(2,1)}) %all-gather.7.cloned.1.call-update) | async-done | bytes 2097168 | tf_op jit(solution)/shard_map/all_gather | solution.py:116
  234.2 5.3 fusion.169
  239.5 45.5 %all-gather.9.cloned.1.call-done = bf16[1024,1024]{1,0:T(8,128)(2,1)} async-done(((bf16[1024,128]{1,0:T(8,128)(2,1)}), bf16[1024,1024]{1,0:T(8,128)(2,1)}) %all-gather.9.cloned.1.call-update) | async-done | bytes 2097168 | tf_op jit(solution)/shard_map/all_gather | solution.py:118
  285.0 10.2 %convert_reduce_fusion.8 = (f32[1024]{0:T(1024)S(1)}, bf16[577,1024]{1,0:T(8,128)(2,1)S(1)}, f32[577,1024]{1,0:T(8,128)}) fusion(f32[577,1024]{1,0:T(8,128)} %fusion.169, f32[1024]{0:T(1024)S(1)} %bitcast.353, bf16[577,1024]{1,0:T(8,128)(2,1)} %get-tuple-element.116, bf16[1024,1024]{1,0:T(8,128)(2,1)} %all-gather.9.cloned.1.call-done), kind=kOutput, calls=%fused_computation.107 | convolution fusion | flops 1254369280 | bytes 9195520 | tf_op jit(solution)/shard_map/rd,fd->rf/dot_general | solution.py:143
  298.9 36.0 %all-reduce.23.cloned.1.call-done = bf16[577,1024]{1,0:T(8,128)(2,1)} async-done(((bf16[577,1024]{1,0:T(8,128)(2,1)}), bf16[577,1024]{1,0:T(8,128)(2,1)}) %all-reduce.23.cloned.1.call-update) | async-done | bytes 1181712 | tf_op jit(solution)/shard_map/psum | solution.py:147
  340.7 8.0 convert_reduce_fusion.9
  353.5 6.5 multiply_convert_fusion.3
  360.0 4.6 convolution_convert_fusion.7
  367.1 23.3 %all-reduce.21.cloned.1.call-done = bf16[577,1024]{1,0:T(8,128)(2,1)} async-done(((bf16[577,1024]{1,0:T(8,128)(2,1)}), bf16[577,1024]{1,0:T(8,128)(2,1)}) %all-reduce.21.cloned.1.call-update) | async-done | bytes 1181712 | tf_op jit(solution)/shard_map/psum | solution.py:147
  390.4 4.9 convert_reduce_fusion.5
  406.0 4.6 convert_reduce_fusion.12
  410.6 7.0 multiply_reduce_fusion
  418.8 4.8 convert_reduce_fusion.14
  423.6 6.8 multiply_reduce_fusion.1
  431.0 4.3 multiply_convert_fusion
  438.3 4.1 multiply_convert_fusion.1
  482.2 4.0 fusion.167
  491.4 22.1 %reduce-scatter.21.cloned.1.call-done = bf16[16,4]{1,0:T(8,128)(2,1)} async-done(((bf16[128,4]{1,0:T(8,128)(2,1)}), bf16[16,4]{1,0:T(8,128)(2,1)}) %reduce-scatter.21.cloned.1.call-update) | async-done | bytes 144
  514.8 64.3 %reduce-scatter.23.cloned.1.call-done = bf16[128,256]{1,0:T(8,128)(2,1)} async-done(((bf16[1024,256]{1,0:T(8,128)(2,1)}), bf16[128,256]{1,0:T(8,128)(2,1)}) %reduce-scatter.23.cloned.1.call-update) | async-done | bytes 65552
  580.7 95.5 %all-reduce.25.cloned.1.call-done = (bf16[577,1024]{1,0:T(8,128)(2,1)}, bf16[577,1024]{1,0:T(8,128)(2,1)}, bf16[577,1024]{1,0:T(8,128)(2,1)}, bf16[577,1024]{1,0:T(8,128)(2,1)}) async-done(((bf16[577,1024]{1,0:T(8,128)(2,1)}, bf16[577,1024]{1,0:T(8,128)(2,1)}, bf16[577,1024]{1,0:T(8,128)(2,1)}, bf16[577,1024]{1,0:T(8,128)(2,1)}), (bf16[577,1024]{1,0:T(8,128)(2,1)}, bf16[577,1024]{1,0:T(8,128)(2,1)}, ...) | async-done | bytes 4726800 | tf_op jit(solution)/shard_map/psum | solution.py:127
  682.3 37.6 %all-reduce.13 = (bf16[1024]{0:T(1024)(128)(2,1)S(1)}, bf16[1024]{0:T(1024)(128)(2,1)S(1)}, bf16[1024]{0:T(1024)(128)(2,1)S(1)}, bf16[1024]{0:T(1024)(128)(2,1)S...) all-reduce(bf16[1024]{0:T(1024)(128)(2,1)S(1)} %add_convert_fusion., ...), channel_id=2, replica_groups=mesh['fsdp'=8,'tensor'=4] {'fsdp'}, use_global_device_ids=true, to_apply=%region_32.0.clone | all-reduce | flops 6144 | bytes 24576
  723.9 5.4 add_bitcast_fusion.1
  735.3 9.4 %copy.96 = f32[2,1,577,1024]{3,1,2,0:T(1,128)} copy(f32[2,1,577,1024]{3,2,1,0:T(8,128)} %pad_maximum_fusion) | data formatting | bytes 9453568
  752.3 63.8 %reduce-scatter.27.cloned.1.call-done = bf16[128,1024]{1,0:T(8,128)(2,1)} async-done(((bf16[1024,1024]{1,0:T(8,128)(2,1)}), bf16[128,1024]{1,0:T(8,128)(2,1)}) %reduce-scatter.27.cloned.1.call-update) | async-done | bytes 262160
  818.0 68.9 %reduce-scatter.17.cloned.1.call-done = bf16[128,1024]{1,0:T(8,128)(2,1)} async-done(((bf16[1024,1024]{1,0:T(8,128)(2,1)}), bf16[128,1024]{1,0:T(8,128)(2,1)}) %reduce-scatter.17.cloned.1.call-update) | async-done | bytes 262160 | tf_op jit(solution)/shard_map/reduce_scatter | solution.py:232
  (301 shorter events, 138.0 us)
Async XLA Ops:
  7.2 106.0 %all-gather.5.cloned.1.call-start = ((), (), s32[]{:S(2)}) async-start(), calls=%async_computation.6 | async-start | bytes 1769472 | tf_op jit(solution)/shard_map/all_gather | solution.py:83
  7.9 174.9 %all-reduce.27.cloned.1.call-start = ((), (), s32[]{:S(2)}) async-start(), calls=%async_computation.18 | async-start | bytes 4784128 | tf_op jit(solution)/shard_map/psum | solution.py:113
  56.2 61.4 %copy-start.54 = (f32[1024]{0:T(1024)}, f32[1024]{0:T(1024)S(1)}, u32[]{:S(2)}) copy-start(f32[1024]{0:T(1024)S(1)} %convert_element_type.440) | copy-start | bytes 12292
  56.2 61.4 %copy-start.39 = (f32[1024]{0:T(1024)}, f32[1024]{0:T(1024)S(1)}, u32[]{:S(2)}) copy-start(f32[1024]{0:T(1024)S(1)} %convert_element_type.439) | copy-start | bytes 12292
  84.5 31.8 %copy-start.43 = (f32[577]{0:T(1024)}, f32[577]{0:T(1024)S(1)}, u32[]{:S(2)}) copy-start(f32[577]{0:T(1024)S(1)} %broadcast_multiply_fusion.3) | copy-start | bytes 6928
  85.0 31.3 %copy-start.46 = (f32[577]{0:T(1024)}, f32[577]{0:T(1024)S(1)}, u32[]{:S(2)}) copy-start(f32[577]{0:T(1024)S(1)} %fusion.36) | copy-start | bytes 6928
  85.0 32.5 %copy-start.41 = (f32[577]{0:T(1024)}, f32[577]{0:T(1024)S(1)}, u32[]{:S(2)}) copy-start(f32[577]{0:T(1024)S(1)} %broadcast_multiply_fusion.1) | copy-start | bytes 6928
  85.5 30.8 %copy-start.48 = (f32[577]{0:T(1024)}, f32[577]{0:T(1024)S(1)}, u32[]{:S(2)}) copy-start(f32[577]{0:T(1024)S(1)} %fusion.34) | copy-start | bytes 6928
  85.6 30.7 %copy-start.52 = (f32[577]{0:T(1024)}, f32[577]{0:T(1024)S(1)}, u32[]{:S(2)}) copy-start(f32[577]{0:T(1024)S(1)} %fusion.158) | copy-start | bytes 6928
  85.6 32.0 %copy-start.50 = (f32[577]{0:T(1024)}, f32[577]{0:T(1024)S(1)}, u32[]{:S(2)}) copy-start(f32[577]{0:T(1024)S(1)} %fusion.160) | copy-start | bytes 6928
  116.3 6.1 copy-start.21
  129.6 104.6 %all-gather.7.cloned.1.call-start = ((), (), s32[]{:S(2)}) async-start(), calls=%async_computation.7 | async-start | bytes 2359296 | tf_op jit(solution)/shard_map/all_gather | solution.py:116
  130.3 154.7 %all-gather.9.cloned.1.call-start = ((), (), s32[]{:S(2)}) async-start(), calls=%async_computation.8 | async-start | bytes 2359296 | tf_op jit(solution)/shard_map/all_gather | solution.py:118
  130.9 204.0 %all-reduce.23.cloned.1.call-start = ((), (), s32[]{:S(2)}) async-start(), calls=%async_computation.10 | async-start | bytes 2392064 | tf_op jit(solution)/shard_map/psum | solution.py:147
  285.0 11.3 %copy-start.60 = (bf16[1024,1024]{1,0:T(8,128)(2,1)S(1)}, bf16[1024,1024]{1,0:T(8,128)(2,1)}, u32[]{:S(2)}) copy-start(bf16[1024,1024]{1,0:T(8,128)(2,1)} %all-gather.7.cloned.1.call-done) | copy-start | bytes 6291460
  298.8 91.6 %all-reduce.21.cloned.1.call-start = ((), (), s32[]{:S(2)}) async-start(), calls=%async_computation.9 | async-start | bytes 2392064 | tf_op jit(solution)/shard_map/psum | solution.py:147
  340.7 8.1 copy-start.27
  352.3 137.7 %reduce-scatter.25.cloned.1.call-start = ((), (), s32[]{:S(2)}) async-start(), calls=%async_computation.15 | async-start | bytes 294912
  360.0 153.5 %reduce-scatter.21.cloned.1.call-start = ((), (), s32[]{:S(2)}) async-start(), calls=%async_computation.13 | async-start | bytes 36864
  390.4 6.6 copy-start.17
  418.7 12.2 %slice-start.2 = ((s8[5980160]{0:T(1024)(128)(4,1)}), s8[4194304]{0:T(1024)(128)(4,1)S(1)}, s32[]{:S(2)}) async-start(s8[5980160]{0:T(1024)(128)(4,1)} %bitcast.331), calls=%async_computation.21 | async-start | bytes 8388608
  423.5 6.8 copy-start.25
  423.5 6.8 copy-start.26
  423.5 7.5 slice-start.3
  431.0 7.4 slice-start
  431.0 7.3 slice-start.1
  435.3 7.1 copy-start.9
  446.3 132.7 %reduce-scatter.23.cloned.1.call-start = ((), (), s32[]{:S(2)}) async-start(), calls=%async_computation.14 | async-start | bytes 589824
  451.2 225.0 %all-reduce.25.cloned.1.call-start = ((), (), s32[]{:S(2)}) async-start(), calls=%async_computation.17 | async-start | bytes 9568256 | tf_op jit(solution)/shard_map/psum | solution.py:127
  460.6 289.8 %reduce-scatter.19.cloned.1.call-start = ((), (), s32[]{:S(2)}) async-start(), calls=%async_computation.12 | async-start | bytes 1769472
  469.5 346.6 %reduce-scatter.27.cloned.1.call-start = ((), (), s32[]{:S(2)}) async-start(), calls=%async_computation.16 | async-start | bytes 2359296
  480.6 406.4 %reduce-scatter.17.cloned.1.call-start = ((), (), s32[]{:S(2)}) async-start(), calls=%async_computation.11 | async-start | bytes 2359296 | tf_op jit(solution)/shard_map/reduce_scatter | solution.py:232
  (53 other events, 175.0 us)
Sparse Core Ops, SparseCore 0:
  10.0 47.7 all-gather.4
  129.7 53.1 all-reduce.26
  185.0 49.1 all-gather.6
  236.1 48.8 all-gather.8
  298.9 35.9 all-reduce.22
  352.4 37.8 all-reduce.20
  393.7 62.2 reduce-scatter.24
  459.7 53.7 reduce-scatter.20
  517.4 61.6 reduce-scatter.22
  582.1 94.1 all-reduce.24
  679.6 65.7 reduce-scatter.18
  748.8 67.2 reduce-scatter.26
  819.6 67.3 reduce-scatter.16
where the time goes:
time: 903 us; the launch traced here: 896 us
  waiting for transfers between devices  495 us (55%)
  blocking collectives  146 us (16%)
  matrix products  115 us (13%)
  other arithmetic  65.3 us (7%)
  local copies, waits for them, and re-layouts  57.5 us (6%)
  between operations  16.2 us (2%)
    unnamed x18, waiting for transfers between devices  152 us
    psum x1, waiting for transfers between devices, shards(): lax.psum(mlp_part.astype(jnp.bfloat16), 'tensor').astype(jnp.float32)  95.5 us
    unnamed x2, blocking collectives  80.7 us
    reduce_scatter x1, waiting for transfers between devices, shards(): lax.psum_scatter(up_acc.astype(jnp.bfloat16), 'fsdp', scatter_dimension=0...  68.9 us
    psum x2, waiting for transfers between devices, shards(): lax.psum(jnp.einsum('rf,df->rd', grad_pre, up_mat, preferred_element_type...  59.3 us
    all_gather x1, waiting for transfers between devices, shards(): lax.all_gather(up_weight, 'fsdp', axis=0, tiled=True)  48.1 us
    all_gather x1, waiting for transfers between devices, shards(): lax.all_gather(down_weight, 'fsdp', axis=1, tiled=True)  45.5 us
    unnamed x169, local copies, waits for them, and re-layouts  38.6 us
  transfers between devices with their start and end apart: 13, of which 10 were waited for; matrix products, arithmetic and copies ran while one was open for 21% of the time, Pallas kernels for 0%

commit v1 on v0

--- a/solution.py
+++ b/solution.py
@@ -124,7 +124,9 @@
         gelu_full, gelu_pull = jax.vjp(gelu_exact, pre_act)
         activated = gelu_full.astype(bf16)
         mlp_part = jnp.dot(activated, down_mat, preferred_element_type=f32)
-        mlp_total = lax.psum(mlp_part.astype(jnp.bfloat16), "tensor").astype(jnp.float32)
+        mlp_total = jnp.sum(lax.all_gather(mlp_part.astype(jnp.bfloat16), "tensor"), axis=0).astype(
+            jnp.float32
+        )
         output_rows = (hidden_res + (mlp_total + down_shift)).astype(bf16)
         outputs_all.append(output_rows.reshape(images_local, seq_len, model_width))
         up_mat, up_shift, down_mat = unpack_mlp(

time: 903 us -> 972 us (1.076)
  waiting for transfers between devices: 495 us -> 551 us
  other arithmetic: 65.3 us -> 75.6 us
    all_gather x0 -> x2, waiting for transfers between devices: none -> 71 us  [shards(): lax.all_gather(mlp_part.astype(jnp.bfloat16), 'tensor')]
    psum x1, waiting for transfers between devices: 95.5 us -> 55.8 us  [shards(): lax.psum(jnp.einsum('rc,dc->rd', grad_proj, qkv_mat, preferred_element_ty...]
    unnamed x18 -> x20, waiting for transfers between devices: 152 us -> 167 us
    psum x2, waiting for transfers between devices: 59.3 us -> 69.3 us  [shards(): lax.psum(jnp.einsum('rf,df->rd', grad_pre, up_mat, preferred_element_type...]
    unnamed x169 -> x171, local copies, waits for them, and re-layouts: 38.6 us -> 38.8 us
  transfers between devices with their start and end apart: 13 -> 15, of which waited for: 10 -> 13; matrix products, arithmetic and copies ran while one was open for 21% -> 17% of each run, Pallas kernels for 0% -> 0%
where the time goes in v1:
time: 972 us; the launch traced here: 965 us
  waiting for transfers between devices  551 us (57%)
  blocking collectives  146 us (15%)
  matrix products  115 us (12%)
  other arithmetic  75.6 us (8%)
  local copies, waits for them, and re-layouts  59.2 us (6%)
  between operations  16 us (2%)
    unnamed x20, waiting for transfers between devices  167 us
    unnamed x2, blocking collectives  80.9 us
    all_gather x2, waiting for transfers between devices, shards(): lax.all_gather(mlp_part.astype(jnp.bfloat16), 'tensor')  71 us
    reduce_scatter x1, waiting for transfers between devices, shards(): lax.psum_scatter(up_acc.astype(jnp.bfloat16), 'fsdp', scatter_dimension=0...  69.7 us
    psum x2, waiting for transfers between devices, shards(): lax.psum(jnp.einsum('rf,df->rd', grad_pre, up_mat, preferred_element_type...  69.3 us
    psum x1, waiting for transfers between devices, shards(): lax.psum(jnp.einsum('rc,dc->rd', grad_proj, qkv_mat, preferred_element_ty...  55.8 us
    all_gather x1, waiting for transfers between devices, shards(): lax.all_gather(up_weight, 'fsdp', axis=0, tiled=True)  48.1 us
    all_gather x1, waiting for transfers between devices, shards(): lax.all_gather(down_weight, 'fsdp', axis=1, tiled=True)  45.4 us
  transfers between devices with their start and end apart: 15, of which 13 were waited for; matrix products, arithmetic and copies ran while one was open for 17% of the time, Pallas kernels for 0%

profile of v1, /device:TPU:0, one launch (start us, length us, event | category | flops | bytes accessed | tf_op | source)
XLA Modules:
  0.0 964.7 jit_solution(11525278804507011988)
XLA Ops:
  13.0 43.2 %all-reduce.12 = (bf16[1024]{0:T(1024)(128)(2,1)S(1)}, bf16[1024]{0:T(1024)(128)(2,1)S(1)}, bf16[1024]{0:T(1024)(128)(2,1)S(1)}, bf16[1024]{0:T(1024)(128)(2,1)S...) all-reduce(bf16[1024]{0:T(1024)(128)(2,1)S(1)} %dynamic-update-slic, ...), channel_id=1, replica_groups=mesh['fsdp'=8,'tensor'=4] {'fsdp','tensor'}, use_global_device_ids=true, to_apply=%add.1 | all-reduce | flops 6144 | bytes 24576
  56.2 21.0 %all-gather.2 = bf16[8,16,4]{1,2,0:T(4,128)(2,1)S(1)} all-gather(bf16[1,16,4]{1,2,0:T(4,128)(2,1)} %bitcast.361), channel_id=1, replica_groups=mesh['fsdp'=8,'tensor'=4] {'fsdp'}, dimensions={0}, use_global_device_ids=true | all-gather | bytes 1152 | tf_op jit(solution)/shard_map/all_gather | solution.py:84
  77.2 6.5 fusion.183
  85.7 27.6 %all_gather.66 = bf16[256,1024]{1,0:T(8,128)(2,1)S(1)} all-gather(bf16[256,128]{1,0:T(8,128)(2,1)S(1)} %copy-done.46), channel_id=1, replica_groups=mesh['fsdp'=8,'tensor'=4] {'fsdp'}, dimensions={1}, use_global_device_ids=true | all-gather | bytes 589824 | tf_op jit(solution)/shard_map/all_gather | solution.py:85
  131.1 16.8 %all_gather.71 = bf16[1,1024]{1,0:T(2,128)(2,1)S(1)} all-gather(bf16[1,128]{1,0:T(2,128)(2,1)S(1)} %copy-done.59), channel_id=1, replica_groups=mesh['fsdp'=8,'tensor'=4] {'fsdp'}, dimensions={1}, use_global_device_ids=true | all-gather | bytes 2304 | tf_op jit(solution)/shard_map/all_gather | solution.py:117
  147.9 7.9 fusion.182
  158.0 24.9 %all-reduce.27.cloned.1.call-done = (bf16[577,1024]{1,0:T(8,128)(2,1)}, bf16[577,1024]{1,0:T(8,128)(2,1)}) async-done(((bf16[577,1024]{1,0:T(8,128)(2,1)}, bf16[577,1024]{1,0:T(8,128)(2,1)}), (bf16[577,1024]{1,0:T(8,128)(2,1)}, bf16[577,1024]{1,0:T(8,128)(2,1)})) %all-reduce.27.cloned.1.call-update) | async-done | bytes 2363408 | tf_op jit(solution)/shard_map/psum | solution.py:113
  186.2 48.1 %all-gather.13.cloned.1.call-done = bf16[1024,1024]{1,0:T(8,128)(2,1)} async-done(((bf16[128,1024]{1,0:T(8,128)(2,1)}), bf16[1024,1024]{1,0:T(8,128)(2,1)}) %all-gather.13.cloned.1.call-update) | async-done | bytes 2097168 | tf_op jit(solution)/shard_map/all_gather | solution.py:116
  234.3 5.4 fusion.171
  239.7 45.4 %all-gather.15.cloned.1.call-done = bf16[1024,1024]{1,0:T(8,128)(2,1)} async-done(((bf16[1024,128]{1,0:T(8,128)(2,1)}), bf16[1024,1024]{1,0:T(8,128)(2,1)}) %all-gather.15.cloned.1.call-update) | async-done | bytes 2097168 | tf_op jit(solution)/shard_map/all_gather | solution.py:118
  285.1 10.2 %convert_reduce_fusion.8 = (f32[1024]{0:T(1024)S(1)}, bf16[577,1024]{1,0:T(8,128)(2,1)S(1)}, f32[577,1024]{1,0:T(8,128)}) fusion(f32[577,1024]{1,0:T(8,128)} %fusion.171, f32[1024]{0:T(1024)S(1)} %bitcast.357, bf16[577,1024]{1,0:T(8,128)(2,1)} %get-tuple-element.114, bf16[1024,1024]{1,0:T(8,128)(2,1)} %all-gather.15.cloned.1.call-done), kind=kOutput, calls=%fused_computation.107 | convolution fusion | flops 1254369280 | bytes 9195520 | tf_op jit(solution)/shard_map/rd,fd->rf/dot_general | solution.py:145
  302.2 32.7 %all-reduce.23.cloned.1.call-done = bf16[577,1024]{1,0:T(8,128)(2,1)} async-done(((bf16[577,1024]{1,0:T(8,128)(2,1)}), bf16[577,1024]{1,0:T(8,128)(2,1)}) %all-reduce.23.cloned.1.call-update) | async-done | bytes 1181712 | tf_op jit(solution)/shard_map/psum | solution.py:149
  340.8 8.0 convert_reduce_fusion.9
  353.9 36.5 %all-reduce.21.cloned.1.call-done = bf16[577,1024]{1,0:T(8,128)(2,1)} async-done(((bf16[577,1024]{1,0:T(8,128)(2,1)}), bf16[577,1024]{1,0:T(8,128)(2,1)}) %all-reduce.21.cloned.1.call-update) | async-done | bytes 1181712 | tf_op jit(solution)/shard_map/psum | solution.py:149
  390.4 4.9 convert_reduce_fusion.5
  410.2 6.9 multiply_reduce_fusion
  418.3 4.8 convert_reduce_fusion.14
  423.1 6.9 multiply_reduce_fusion.1
  469.3 5.2 multiply_convert_fusion.3
  503.7 9.9 %reduce-scatter.21.cloned.1.call-done = bf16[16,4]{1,0:T(8,128)(2,1)} async-done(((bf16[128,4]{1,0:T(8,128)(2,1)}), bf16[16,4]{1,0:T(8,128)(2,1)}) %reduce-scatter.21.cloned.1.call-update) | async-done | bytes 144
  514.9 64.3 %reduce-scatter.23.cloned.1.call-done = bf16[128,256]{1,0:T(8,128)(2,1)} async-done(((bf16[1024,256]{1,0:T(8,128)(2,1)}), bf16[128,256]{1,0:T(8,128)(2,1)}) %reduce-scatter.23.cloned.1.call-update) | async-done | bytes 65552
  580.8 55.8 %all-reduce.25.cloned.1.call-done = (bf16[577,1024]{1,0:T(8,128)(2,1)}, bf16[577,1024]{1,0:T(8,128)(2,1)}) async-done(((bf16[577,1024]{1,0:T(8,128)(2,1)}, bf16[577,1024]{1,0:T(8,128)(2,1)}), (bf16[577,1024]{1,0:T(8,128)(2,1)}, bf16[577,1024]{1,0:T(8,128)(2,1)})) %all-reduce.25.cloned.1.call-update) | async-done | bytes 2363408 | tf_op jit(solution)/shard_map/psum | solution.py:209
  642.8 37.8 %all-reduce.13 = (bf16[1024]{0:T(1024)(128)(2,1)S(1)}, bf16[1024]{0:T(1024)(128)(2,1)S(1)}, bf16[1024]{0:T(1024)(128)(2,1)S(1)}, bf16[1024]{0:T(1024)(128)(2,1)S...) all-reduce(bf16[1024]{0:T(1024)(128)(2,1)S(1)} %add_convert_fusion., ...), channel_id=4, replica_groups=mesh['fsdp'=8,'tensor'=4] {'fsdp'}, use_global_device_ids=true, to_apply=%region_32.0.clone | all-reduce | flops 6144 | bytes 24576
  684.5 21.5 %reduce-scatter.19.cloned.1.call-done = bf16[128,768]{1,0:T(8,128)(2,1)} async-done(((bf16[1024,768]{1,0:T(8,128)(2,1)}), bf16[128,768]{1,0:T(8,128)(2,1)}) %reduce-scatter.19.cloned.1.call-update) | async-done | bytes 196624
  707.9 69.3 %reduce-scatter.27.cloned.1.call-done = bf16[128,1024]{1,0:T(8,128)(2,1)} async-done(((bf16[1024,1024]{1,0:T(8,128)(2,1)}), bf16[128,1024]{1,0:T(8,128)(2,1)}) %reduce-scatter.27.cloned.1.call-update) | async-done | bytes 262160
  779.2 69.7 %reduce-scatter.17.cloned.1.call-done = bf16[128,1024]{1,0:T(8,128)(2,1)} async-done(((bf16[1024,1024]{1,0:T(8,128)(2,1)}), bf16[128,1024]{1,0:T(8,128)(2,1)}) %reduce-scatter.17.cloned.1.call-update) | async-done | bytes 262160 | tf_op jit(solution)/shard_map/reduce_scatter | solution.py:234
  850.6 36.6 %all-gather.19.cloned.1.call-done = bf16[4,577,1024]{2,1,0:T(8,128)(2,1)} async-done(((bf16[1,577,1024]{2,1,0:T(8,128)(2,1)}), bf16[4,577,1024]{2,1,0:T(8,128)(2,1)}) %all-gather.19.cloned.1.call-update) | async-done | bytes 4726800 | tf_op jit(solution)/shard_map/all_gather | solution.py:127
  887.2 4.8 reduce_sum.379
  892.0 34.4 %all-gather.17.cloned.1.call-done = bf16[4,577,1024]{2,1,0:T(8,128)(2,1)} async-done(((bf16[1,577,1024]{2,1,0:T(8,128)(2,1)}), bf16[4,577,1024]{2,1,0:T(8,128)(2,1)}) %all-gather.17.cloned.1.call-update) | async-done | bytes 4726800 | tf_op jit(solution)/shard_map/all_gather | solution.py:127
  926.5 4.8 reduce_sum.370
  931.3 5.4 add_bitcast_fusion.1
  942.9 9.4 copy.96
  (311 shorter events, 162.1 us)
Async XLA Ops:
  7.2 106.1 %all-gather.11.cloned.1.call-start = ((), (), s32[]{:S(2)}) async-start(), calls=%async_computation.6 | async-start | bytes 1769472 | tf_op jit(solution)/shard_map/all_gather | solution.py:83
  7.9 175.0 %all-reduce.27.cloned.1.call-start = ((), (), s32[]{:S(2)}) async-start(), calls=%async_computation.20 | async-start | bytes 4784128 | tf_op jit(solution)/shard_map/psum | solution.py:113
  56.2 61.5 %copy-start.56 = (f32[1024]{0:T(1024)}, f32[1024]{0:T(1024)S(1)}, u32[]{:S(2)}) copy-start(f32[1024]{0:T(1024)S(1)} %convert_element_type.444) | copy-start | bytes 12292
  56.2 61.5 %copy-start.40 = (f32[1024]{0:T(1024)}, f32[1024]{0:T(1024)S(1)}, u32[]{:S(2)}) copy-start(f32[1024]{0:T(1024)S(1)} %convert_element_type.443) | copy-start | bytes 12292
  84.6 31.8 %copy-start.44 = (f32[577]{0:T(1024)}, f32[577]{0:T(1024)S(1)}, u32[]{:S(2)}) copy-start(f32[577]{0:T(1024)S(1)} %broadcast_multiply_fusion.3) | copy-start | bytes 6928
  85.1 31.4 %copy-start.47 = (f32[577]{0:T(1024)}, f32[577]{0:T(1024)S(1)}, u32[]{:S(2)}) copy-start(f32[577]{0:T(1024)S(1)} %fusion.36) | copy-start | bytes 6928
  85.1 32.6 %copy-start.42 = (f32[577]{0:T(1024)}, f32[577]{0:T(1024)S(1)}, u32[]{:S(2)}) copy-start(f32[577]{0:T(1024)S(1)} %broadcast_multiply_fusion.1) | copy-start | bytes 6928
  85.5 30.9 %copy-start.49 = (f32[577]{0:T(1024)}, f32[577]{0:T(1024)S(1)}, u32[]{:S(2)}) copy-start(f32[577]{0:T(1024)S(1)} %fusion.34) | copy-start | bytes 6928
  85.6 30.8 %copy-start.53 = (f32[577]{0:T(1024)}, f32[577]{0:T(1024)S(1)}, u32[]{:S(2)}) copy-start(f32[577]{0:T(1024)S(1)} %fusion.160) | copy-start | bytes 6928
  85.7 32.0 %copy-start.51 = (f32[577]{0:T(1024)}, f32[577]{0:T(1024)S(1)}, u32[]{:S(2)}) copy-start(f32[577]{0:T(1024)S(1)} %fusion.162) | copy-start | bytes 6928
  129.7 104.6 %all-gather.13.cloned.1.call-start = ((), (), s32[]{:S(2)}) async-start(), calls=%async_computation.7 | async-start | bytes 2359296 | tf_op jit(solution)/shard_map/all_gather | solution.py:116
  130.4 154.7 %all-gather.15.cloned.1.call-start = ((), (), s32[]{:S(2)}) async-start(), calls=%async_computation.8 | async-start | bytes 2359296 | tf_op jit(solution)/shard_map/all_gather | solution.py:118
  131.0 204.0 %all-reduce.23.cloned.1.call-start = ((), (), s32[]{:S(2)}) async-start(), calls=%async_computation.10 | async-start | bytes 2392064 | tf_op jit(solution)/shard_map/psum | solution.py:149
  285.1 11.3 %copy-start.61 = (bf16[1024,1024]{1,0:T(8,128)(2,1)S(1)}, bf16[1024,1024]{1,0:T(8,128)(2,1)}, u32[]{:S(2)}) copy-start(bf16[1024,1024]{1,0:T(8,128)(2,1)} %all-gather.13.cloned.1.call-done) | copy-start | bytes 6291460
  298.8 91.6 %all-reduce.21.cloned.1.call-start = ((), (), s32[]{:S(2)}) async-start(), calls=%async_computation.9 | async-start | bytes 2392064 | tf_op jit(solution)/shard_map/psum | solution.py:149
  340.8 8.0 copy-start.29
  352.4 149.9 %reduce-scatter.25.cloned.1.call-start = ((), (), s32[]{:S(2)}) async-start(), calls=%async_computation.17 | async-start | bytes 294912
  353.4 160.2 %reduce-scatter.21.cloned.1.call-start = ((), (), s32[]{:S(2)}) async-start(), calls=%async_computation.15 | async-start | bytes 36864
  418.3 12.3 %slice-start.2 = ((s8[5980160]{0:T(1024)(128)(4,1)}), s8[4194304]{0:T(1024)(128)(4,1)S(1)}, s32[]{:S(2)}) async-start(s8[5980160]{0:T(1024)(128)(4,1)} %bitcast.335), calls=%async_computation.23 | async-start | bytes 8388608
  423.1 6.9 copy-start.26
  423.1 6.9 copy-start.28
  423.1 7.5 slice-start.3
  430.6 7.4 slice-start
  430.6 7.3 slice-start.1
  434.9 7.1 copy-start.9
  446.0 133.3 %reduce-scatter.23.cloned.1.call-start = ((), (), s32[]{:S(2)}) async-start(), calls=%async_computation.16 | async-start | bytes 589824
  450.8 185.8 %all-reduce.25.cloned.1.call-start = ((), (), s32[]{:S(2)}) async-start(), calls=%async_computation.19 | async-start | bytes 4784128 | tf_op jit(solution)/shard_map/psum | solution.py:209
  460.3 245.8 %reduce-scatter.19.cloned.1.call-start = ((), (), s32[]{:S(2)}) async-start(), calls=%async_computation.14 | async-start | bytes 1769472
  469.2 308.0 %reduce-scatter.27.cloned.1.call-start = ((), (), s32[]{:S(2)}) async-start(), calls=%async_computation.18 | async-start | bytes 2359296
  483.9 365.0 %reduce-scatter.17.cloned.1.call-start = ((), (), s32[]{:S(2)}) async-start(), calls=%async_computation.11 | async-start | bytes 2359296 | tf_op jit(solution)/shard_map/reduce_scatter | solution.py:234
  491.9 395.3 %all-gather.19.cloned.1.call-start = ((), (), s32[]{:S(2)}) async-start(), calls=%async_computation.13 | async-start | bytes 5980160 | tf_op jit(solution)/shard_map/all_gather | solution.py:127
  496.4 430.0 %all-gather.17.cloned.1.call-start = ((), (), s32[]{:S(2)}) async-start(), calls=%async_computation.12 | async-start | bytes 5980160 | tf_op jit(solution)/shard_map/all_gather | solution.py:127
  (56 other events, 188.3 us)
Sparse Core Ops, SparseCore 0:
  10.0 47.7 all-gather.10
  129.8 53.1 all-reduce.26
  185.1 49.1 all-gather.12
  236.2 48.8 all-gather.14
  299.0 35.9 all-reduce.22
  352.5 37.8 all-reduce.20
  393.7 62.2 reduce-scatter.24
  459.7 53.8 reduce-scatter.20
  517.5 61.6 reduce-scatter.22
  581.4 55.1 all-reduce.24
  640.1 65.9 reduce-scatter.18
  710.0 67.1 reduce-scatter.26
  781.3 67.4 reduce-scatter.16
  850.3 36.8 all-gather.18
  888.6 37.7 all-gather.16
